TPU v7x, 32 devices: a whole 2x2x4 slice. The times are simulated.
32 devices in a mesh: dp: 8 (over y, x, core), tensor: 4 (over z).
Axes of the slice: x: 2, y: 2, z: 4, core: 2. Of those that a mesh axis runs over, the one named last changes fastest.
Arguments:
- inputs: float32 [8192, 1536], P(('dp', 'tensor')), may hold values from -80 to 80
- norm_gains: float32 [1, 2, 1536], replicated, may hold values from 0.5 to 1.5
- w_qkv: bfloat16 [1, 1536, 3072], P(None, 'dp', 'tensor'), may hold values from -0.15625 to 0.15625
- w_gate_up: bfloat16 [1, 1536, 2, 4096], P(None, 'dp', None, 'tensor'), may hold values from -0.15625 to 0.15625
- w_out: bfloat16 [1, 1536, 1536], P(None, 'dp', 'tensor'), may hold values from -2.5 to 2.5
- w_down: bfloat16 [1, 1536, 4096], P(None, 'dp', 'tensor'), may hold values from -0.09375 to 0.09375
- segments: int32 [8192], P('dp'), may hold values from 0 to 8, as said below
- positions: int32 [8192], P('dp'), may hold values from 0 to 799, as said below
- cotangent: bfloat16 [8192, 1536], P(('dp', 'tensor')), may hold values from -6 to 6
Outputs:
- output: float32 [8192, 1536], P(('dp', 'tensor'))
- input_grad: float32 [8192, 1536], P(('dp', 'tensor'))
- grad_qkv: float32 [1, 1536, 3072], P(None, 'dp', 'tensor')
- grad_gate_up: float32 [1, 1536, 2, 4096], P(None, 'dp', None, 'tensor')
- grad_out: float32 [1, 1536, 1536], P(None, 'dp', 'tensor')
- grad_down: float32 [1, 1536, 4096], P(None, 'dp', 'tensor')
- grad_gains: float32 [1, 2, 1536], replicated
- rms_stats: float32 [1, 4], replicated
Inputs may be any that keep to these rules, and one draw needn't show every extreme that they name: `segments`: within each group of 1024 consecutive tokens (one index of dp), the tokens form blocks of 32: 24 prompt blocks with segment 0 and one block for each continuation 1 to 8, in a drawn order of blocks. Within a group the prompt's tokens have positions 0 to 767, rising along the group; each continuation's tokens have positions 768 to 799 in order.
All inputs are finite; a program needn't handle non-finite values.
Results may differ from a plain program's by a relative error of at most 0.012.
The roundings to bfloat16 on the way count: a program that leaves them out, or rounds other values in their place, can miss the bound.
Values may be sent and summed in bfloat16 or wider, within the bound.
A program may use at most 192 MiB of HBM per device.

v0:
```python
import jax
import jax.numpy as jnp
from jax import lax
from jax.sharding import PartitionSpec as P

HEADS = 16
KV_HEADS = 8
HEAD_WIDTH = 96
norm_eps = 1e-05
rope_base = 100000.0


def rope_tables(position, head_dim):
    freq_steps = jnp.arange(head_dim // 2, dtype=jnp.float32) * (2.0 / head_dim)
    inverse = jnp.power(rope_base, -freq_steps)
    angles = position.astype(jnp.float32)[:, None] * inverse[None, :]
    return (jnp.cos(angles), jnp.sin(angles))


def rotate(values, cosine_table, sine_table):
    half_dim = values.shape[-1] // 2
    first_half = values[..., :half_dim]
    second_half = values[..., half_dim:]
    return jnp.concatenate(
        [
            first_half * cosine_table - second_half * sine_table,
            second_half * cosine_table + first_half * sine_table,
        ],
        axis=-1,
    )


def visible(query_segment, query_position, key_segment, key_position):
    same_doc = (key_segment[None, :] == 0) | (key_segment[None, :] == query_segment[:, None])
    return same_doc & (key_position[None, :] <= query_position[:, None])


def normalize(values, gain):
    inverse = lax.rsqrt(jnp.mean(values * values, axis=-1, keepdims=True) + norm_eps)
    return (values * inverse * gain, inverse)


def norm_back(values, inverse, gain, grad_normed):
    scaled = grad_normed * gain
    grad_gain = jnp.sum(grad_normed * values * inverse, axis=0)
    grad_values = inverse * scaled - values * inverse**3 * jnp.mean(
        scaled * values, axis=-1, keepdims=True
    )
    return (grad_values, grad_gain)


def spread_rows(values):
    return lax.all_gather(values, "tensor", axis=0, tiled=True)


def collect_rows(values):
    return lax.psum_scatter(values, "tensor", scatter_dimension=0, tiled=True)


def spread_grads(values):
    return lax.all_gather(values, "tensor", axis=0, tiled=True)


def collect_grads(values):
    return lax.psum_scatter(values, "tensor", scatter_dimension=0, tiled=True)


def refold(normed_local, grad_rows):
    return jnp.einsum(
        "td,tc->dc",
        lax.all_gather(normed_local, "tensor", axis=0, tiled=True),
        grad_rows,
        preferred_element_type=jnp.float32,
    )


def per_device(inputs, norm_gains, w_qkv, w_gate_up, w_out, w_down, segments, positions, cotangent):
    layers = w_qkv.shape[0]
    head_dim = HEAD_WIDTH
    repeat = HEADS // KV_HEADS
    kv_local = w_out.shape[2] // (repeat * head_dim)
    ff_local = w_down.shape[2]
    group_len = segments.shape[0]
    blocks = 2
    block_len = group_len // blocks
    score_scale = head_dim ** (-0.5)
    cosine_table, sine_table = rope_tables(positions, head_dim)
    cosine_wide = cosine_table[:, None, None, :]
    sine_wide = sine_table[:, None, None, :]
    block_segments = segments.reshape(blocks, block_len)
    block_positions = positions.reshape(blocks, block_len)
    layer_index = 0
    gathered = (
        lax.all_gather(w_qkv[layer_index], "dp", axis=0, tiled=True),
        lax.all_gather(w_gate_up[layer_index], "dp", axis=0, tiled=True),
        lax.all_gather(w_out[layer_index], "dp", axis=0, tiled=True),
        lax.all_gather(w_down[layer_index], "dp", axis=0, tiled=True),
    )
    qkv_full, gate_up_full, out_full, down_full = gathered
    normed_one, inverse_one = normalize(inputs, norm_gains[layer_index, 0])
    normed_one = normed_one.astype(jnp.bfloat16)
    normed_rows = spread_rows(normed_one)
    joined_rows = jnp.dot(normed_rows, qkv_full, preferred_element_type=jnp.float32)
    joined_rows = joined_rows.reshape(group_len, kv_local, repeat + 2, head_dim)
    query_matrix = rotate(joined_rows[:, :, :repeat], cosine_wide, sine_wide).astype(jnp.bfloat16)
    key_matrix = rotate(joined_rows[:, :, repeat], cosine_wide[:, :, 0], sine_wide[:, :, 0]).astype(
        jnp.bfloat16
    )
    value_matrix = joined_rows[:, :, repeat + 1].astype(jnp.bfloat16)

    def attend_block(block_item):
        query_block, block_segment, block_position = block_item
        allowed = visible(block_segment, block_position, segments, positions)
        attention_scores = (
            jnp.einsum(
                "mely,cey->elmc", query_block, key_matrix, preferred_element_type=jnp.float32
            )
            * score_scale
        )
        attention_scores = jnp.where(allowed[None, None], attention_scores, -1e30)
        row_top = jnp.max(attention_scores, axis=-1, keepdims=True)
        weights = jnp.exp(attention_scores - row_top)
        row_total = jnp.sum(weights, axis=-1, keepdims=True)
        probability_lowered = (weights / row_total).astype(jnp.bfloat16)
        mixed_rows_block = jnp.einsum(
            "zbvq,qzo->vzbo", probability_lowered, value_matrix, preferred_element_type=jnp.float32
        )
        return (mixed_rows_block.astype(jnp.bfloat16), (row_top + jnp.log(row_total))[..., 0])

    mixed_all, log_sums = lax.map(
        attend_block,
        (
            query_matrix.reshape(blocks, block_len, kv_local, repeat, head_dim),
            block_segments,
            block_positions,
        ),
    )
    attended = mixed_all.reshape(group_len, kv_local * repeat * head_dim)
    branch = collect_rows(
        jnp.einsum("tk,dk->td", attended, out_full, preferred_element_type=jnp.float32)
    )
    middle = inputs + branch
    normed_two, inverse_two = normalize(middle, norm_gains[layer_index, 1])
    normed_two = normed_two.astype(jnp.bfloat16)
    ff_kept = None
    normed_rows_two = spread_rows(normed_two)
    gate_up = jnp.einsum(
        "td,dcf->tcf", normed_rows_two, gate_up_full, preferred_element_type=jnp.float32
    )
    product = (jax.nn.silu(gate_up[:, 0]) * gate_up[:, 1]).astype(jnp.bfloat16)
    branch_two = collect_rows(
        jnp.einsum("tf,df->td", product, down_full, preferred_element_type=jnp.float32)
    )
    output = middle + branch_two
    stat_rows = [
        jnp.stack(
            [
                jnp.sum(middle * middle),
                jnp.sum(output * output),
                jnp.sum(branch * branch),
                jnp.sum(branch_two * branch_two),
            ]
        )
    ]
    kept_items = [
        (
            inputs,
            inverse_one,
            normed_one,
            normed_rows,
            middle,
            inverse_two,
            normed_two,
            normed_rows_two,
            query_matrix,
            key_matrix,
            value_matrix,
            attended,
            log_sums,
            gate_up,
            product,
            gathered,
            ff_kept,
        )
    ]
    grad_hidden = cotangent.astype(jnp.float32)
    grad_qkv_list = [None] * layers
    grad_gu_list = [None] * layers
    grad_out_list = [None] * layers
    grad_down_list = [None] * layers
    gain_list = [None] * layers
    for layer_index in reversed(range(layers)):
        (
            hidden_in,
            inverse_one,
            normed_one,
            normed_rows,
            middle,
            inverse_two,
            normed_two,
            normed_rows_two,
            query_matrix,
            key_matrix,
            value_matrix,
            attended,
            log_sums,
            gate_up,
            product,
            gathered,
            ff_kept,
        ) = kept_items[layer_index]
        qkv_full, gate_up_full, out_full, down_full = (
            lax.all_gather(w_qkv[layer_index], "dp", axis=0, tiled=True),
            lax.all_gather(w_gate_up[layer_index], "dp", axis=0, tiled=True),
            lax.all_gather(w_out[layer_index], "dp", axis=0, tiled=True),
            lax.all_gather(w_down[layer_index], "dp", axis=0, tiled=True),
        )
        gate_rows = gate_up[:, 0]
        up_rows = gate_up[:, 1]
        sigmoid_gate = jax.nn.sigmoid(gate_rows)
        grad_two = spread_grads(grad_hidden.astype(jnp.bfloat16))
        grad_product = jnp.einsum(
            "td,df->tf", grad_two, down_full, preferred_element_type=jnp.float32
        )
        grad_down_w = jnp.einsum("td,tf->df", grad_two, product, preferred_element_type=jnp.float32)
        grad_gate = (
            grad_product * up_rows * (sigmoid_gate * (1.0 + gate_rows * (1.0 - sigmoid_gate)))
        )
        grad_up = grad_product * (gate_rows * sigmoid_gate)
        grad_gate_up = jnp.stack([grad_gate, grad_up], axis=1).astype(jnp.bfloat16)
        grad_gu_w = refold(normed_two, grad_gate_up.reshape(group_len, 2 * ff_local)).reshape(
            -1, 2, ff_local
        )
        grad_normed_two = collect_grads(
            jnp.einsum(
                "tcf,dcf->td", grad_gate_up, gate_up_full, preferred_element_type=jnp.float32
            )
        )
        grad_middle, grad_gain_two = norm_back(
            middle, inverse_two, norm_gains[layer_index, 1], grad_normed_two
        )
        grad_middle = grad_middle + grad_hidden
        grad_one = spread_grads(grad_middle.astype(jnp.bfloat16))
        grad_attended = jnp.einsum(
            "td,dk->tk", grad_one, out_full, preferred_element_type=jnp.float32
        ).astype(jnp.bfloat16)
        grad_out_w = jnp.einsum("td,tk->dk", grad_one, attended, preferred_element_type=jnp.float32)

        def back_block(running_grads, block_item):
            grad_keys, grad_values = running_grads
            query_block, block_gradient, block_sums, block_segment, block_position = block_item
            allowed = visible(block_segment, block_position, segments, positions)
            attention_scores = (
                jnp.einsum(
                    "mely,cey->elmc", query_block, key_matrix, preferred_element_type=jnp.float32
                )
                * score_scale
            )
            attention_scores = jnp.where(allowed[None, None], attention_scores, -1e30)
            probability_full = jnp.exp(attention_scores - block_sums[..., None])
            grad_probs = jnp.einsum(
                "mely,cey->elmc", block_gradient, value_matrix, preferred_element_type=jnp.float32
            )
            row_delta = jnp.sum(probability_full * grad_probs, axis=-1, keepdims=True)
            score_gradient = (probability_full * (grad_probs - row_delta)).astype(jnp.bfloat16)
            grad_query = (
                jnp.einsum(
                    "zbvq,qzo->vzbo", score_gradient, key_matrix, preferred_element_type=jnp.float32
                )
                * score_scale
            )
            grad_keys = (
                grad_keys
                + jnp.einsum(
                    "wqpv,pwqo->vwo",
                    score_gradient,
                    query_block,
                    preferred_element_type=jnp.float32,
                )
                * score_scale
            )
            grad_values = grad_values + jnp.einsum(
                "wqpv,pwqo->vwo",
                probability_full.astype(jnp.bfloat16),
                block_gradient,
                preferred_element_type=jnp.float32,
            )
            return ((grad_keys, grad_values), grad_query)

        zero_rows = jnp.zeros((group_len, kv_local, head_dim), jnp.float32)
        (grad_keys, grad_values), grad_query = lax.scan(
            back_block,
            (zero_rows, zero_rows),
            (
                query_matrix.reshape(blocks, block_len, kv_local, repeat, head_dim),
                grad_attended.reshape(blocks, block_len, kv_local, repeat, head_dim),
                log_sums,
                block_segments,
                block_positions,
            ),
        )
        grad_query = rotate(
            grad_query.reshape(group_len, kv_local, repeat, head_dim), cosine_wide, -sine_wide
        )
        grad_keys = rotate(grad_keys, cosine_wide[:, :, 0], -sine_wide[:, :, 0])
        grad_joined = jnp.concatenate(
            [grad_query, grad_keys[:, :, None], grad_values[:, :, None]], axis=2
        )
        grad_joined = grad_joined.reshape(group_len, kv_local * (repeat + 2) * head_dim).astype(
            jnp.bfloat16
        )
        grad_qkv_w = refold(normed_one, grad_joined)
        grad_normed_one = collect_grads(
            jnp.einsum("tc,dc->td", grad_joined, qkv_full, preferred_element_type=jnp.float32)
        )
        grad_input, grad_gain_one = norm_back(
            hidden_in, inverse_one, norm_gains[layer_index, 0], grad_normed_one
        )
        grad_hidden = grad_input + grad_middle
        shards = (
            lax.psum_scatter(grad_qkv_w, "dp", scatter_dimension=0, tiled=True),
            lax.psum_scatter(grad_gu_w, "dp", scatter_dimension=0, tiled=True),
            lax.psum_scatter(grad_out_w, "dp", scatter_dimension=0, tiled=True),
            lax.psum_scatter(grad_down_w, "dp", scatter_dimension=0, tiled=True),
        )
        grad_qkv_list[layer_index] = shards[0]
        grad_gu_list[layer_index] = shards[1]
        grad_out_list[layer_index] = shards[2]
        grad_down_list[layer_index] = shards[3]
        gain_list[layer_index] = jnp.stack([grad_gain_one, grad_gain_two])
    gain_total, stat_total = lax.psum(
        (jnp.stack(gain_list), jnp.stack(stat_rows)), ("dp", "tensor")
    )
    cell_count = inputs.shape[0] * inputs.shape[1] * lax.axis_size("dp") * lax.axis_size("tensor")
    rms_values = jnp.sqrt(stat_total / cell_count)
    return (
        output,
        grad_hidden,
        jnp.stack(grad_qkv_list),
        jnp.stack(grad_gu_list),
        jnp.stack(grad_out_list),
        jnp.stack(grad_down_list),
        gain_total,
        rms_values,
    )


def solution(mesh):
    placed = (
        P(("dp", "tensor"), None),
        P(),
        P(None, "dp", "tensor"),
        P(None, "dp", None, "tensor"),
        P(None, "dp", "tensor"),
        P(None, "dp", "tensor"),
        P("dp"),
        P("dp"),
        P(("dp", "tensor"), None),
    )
    return jax.shard_map(
        per_device,
        mesh=mesh,
        in_specs=placed,
        out_specs=(
            P(("dp", "tensor"), None),
            P(("dp", "tensor"), None),
            P(None, "dp", "tensor"),
            P(None, "dp", None, "tensor"),
            P(None, "dp", "tensor"),
            P(None, "dp", "tensor"),
            P(),
            P(),
        ),
        check_vma=False,
    )
```

profile of v0, /device:TPU:0, one launch (start us, length us, event | category | flops | bytes accessed | tf_op | source)
XLA Modules:
  0.0 1162.8 jit_solution(16583962716732105338)
XLA Ops:
  11.0 2.5 multiply_convert_fusion.2
  15.8 25.8 %all-gather.21.cloned.1.call-done = bf16[1,1536,768]{2,1,0:T(8,128)(2,1)} async-done(((bf16[1,192,768]{2,1,0:T(8,128)(2,1)}), bf16[1,1536,768]{2,1,0:T(8,128)(2,1)}) %all-gather.21.cloned.1.call-update) | async-done | bytes 2359312 | tf_op jit(solution)/shard_map/all_gather | solution.py:94
  41.7 65.7 %all-gather.13.cloned.1.call-done = bf16[1024,1536]{1,0:T(8,128)(2,1)} async-done(((bf16[256,1536]{1,0:T(8,128)(2,1)}), bf16[1024,1536]{1,0:T(8,128)(2,1)}) %all-gather.13.cloned.1.call-update) | async-done | bytes 3145744 | tf_op jit(solution)/shard_map/all_gather | solution.py:53
  107.3 5.3 fusion.69
  115.7 18.8 %while.27 = (s32[]{:T(128)}, bf16[2,512,2,2,96]{1,4,3,2,0:T(8,128)(2,1)S(1)}, f32[2,2,2,512]{3,2,1,0:T(2,128)}, s32[1024]{0:T(1024)S(1)}, s32[2,512]{1,0:T(2,128...) while((s32[]{:T(128)}, ...), condition=%wide.region_4.5_spmd, body=%wide.region_1.4_spmd.sunk | while | flops 832764928 | bytes 28928132 | solution.py:130
  121.0 3.7 fusion.116
  130.1 3.7 fusion.116
  135.5 6.0 fusion.72
  142.1 108.9 %reduce-scatter.11.cloned.1.call-done = f32[256,1536]{1,0:T(8,128)} async-done(((f32[1024,1536]{1,0:T(8,128)}), f32[256,1536]{1,0:T(8,128)}) %reduce-scatter.11.cloned.1.call-update) | async-done | bytes 1572880 | tf_op jit(solution)/shard_map/reduce_scatter | solution.py:57
  251.1 2.5 multiply_reduce_fusion.9
  257.4 41.5 %all-gather.25.cloned.1.call-done = bf16[1,1536,2,1024]{3,2,0,1:T(2,128)(2,1)} async-done(((bf16[1,192,2,1024]{3,2,0,1:T(2,128)(2,1)}), bf16[1,1536,2,1024]{3,2,0,1:T(2,128)(2,1)}) %all-gather.25.cloned.1.call-update) | async-done | bytes 6291472 | tf_op jit(solution)/shard_map/all_gather | solution.py:95
  298.9 16.5 %copy.45 = bf16[1,1536,2,1024]{1,3,2,0:T(8,128)(2,1)} copy(bf16[1,1536,2,1024]{3,2,0,1:T(2,128)(2,1)} %all-gather.25.cloned.1.call-done) | data formatting | bytes 12582912 | tf_op jit(solution)/shard_map/all_gather | solution.py:95
  315.3 49.1 %all-gather.15.cloned.1.call-done = bf16[1024,1536]{1,0:T(8,128)(2,1)} async-done(((bf16[256,1536]{1,0:T(8,128)(2,1)}), bf16[1024,1536]{1,0:T(8,128)(2,1)}) %all-gather.15.cloned.1.call-update) | async-done | bytes 3145744 | tf_op jit(solution)/shard_map/all_gather | solution.py:53
  364.4 11.7 %fusion.53 = f32[1024,2,1024]{0,2,1:T(8,128)} fusion(bf16[1,1536,2,1024]{1,3,2,0:T(8,128)(2,1)} %copy.45, bf16[1024,1536]{1,0:T(8,128)(2,1)} %all-gather.15.cloned.1.call-done), kind=kOutput, calls=%fused_computation.68 | convolution fusion | flops 6442450944 | bytes 17825792 | tf_op jit(solution)/shard_map/td,dcf->tcf/dot_general | solution.py:147
  376.1 52.0 %all-gather.17.cloned.1.call-done = bf16[1024,1536]{1,0:T(8,128)(2,1)} async-done(((bf16[256,1536]{1,0:T(8,128)(2,1)}), bf16[1024,1536]{1,0:T(8,128)(2,1)}) %all-gather.17.cloned.1.call-update) | async-done | bytes 3145744 | tf_op jit(solution)/shard_map/all_gather | solution.py:61
  428.1 32.9 %all-gather.27.cloned.1.call-done = bf16[1,1536,1024]{2,1,0:T(8,128)(2,1)} async-done(((bf16[1,192,1024]{2,1,0:T(8,128)(2,1)}), bf16[1,1536,1024]{2,1,0:T(8,128)(2,1)}) %all-gather.27.cloned.1.call-update) | async-done | bytes 3145744 | tf_op jit(solution)/shard_map/all_gather | solution.py:97
  461.0 10.2 multiply_bitcast_fusion.1
  473.2 10.8 fusion.55
  484.3 5.0 multiply_convert_fusion
  490.7 5.4 fusion.63
  496.2 98.7 %reduce-scatter.15.cloned.1.call-done = f32[256,1536]{1,0:T(8,128)} async-done(((f32[1024,1536]{1,0:T(8,128)}), f32[256,1536]{1,0:T(8,128)}) %reduce-scatter.15.cloned.1.call-update) | async-done | bytes 1572880 | tf_op jit(solution)/shard_map/reduce_scatter | solution.py:65
  594.9 2.8 multiply_reduce_fusion.3
  598.4 110.0 %reduce-scatter.13.cloned.1.call-done = f32[256,1536]{1,0:T(8,128)} async-done(((f32[1024,1536]{1,0:T(8,128)}), f32[256,1536]{1,0:T(8,128)}) %reduce-scatter.13.cloned.1.call-update) | async-done | bytes 1572880 | tf_op jit(solution)/shard_map/reduce_scatter | solution.py:57
  708.4 5.4 multiply_reduce_fusion.2
  713.9 8.6 convolution_bitcast_fusion.1
  722.4 6.7 copy.69
  730.7 11.7 %fusion.58 = f32[1536,2,1024]{2,0,1:T(8,128)} fusion(bf16[1024,1536]{1,0:T(8,128)(2,1)} %all-gather.15.cloned.1.call-done, bf16[1024,1,1024]{0,2,1:T(8,128)(2,1)} %copy-done.26, bf16[1024,1,1024]{0,2,1:T(8,128)(2,1)S(1)} %copy-done.25), kind=kOutput, calls=%fused_computation.74 | convolution fusion | flops 6450839552 | bytes 19922944 | tf_op jit(solution)/shard_map/td,tc->dc/dot_general | solution.py:69
  742.5 35.5 %all-gather.19.cloned.1.call-done = bf16[1024,1536]{1,0:T(8,128)(2,1)} async-done(((bf16[256,1536]{1,0:T(8,128)(2,1)}), bf16[1024,1536]{1,0:T(8,128)(2,1)}) %all-gather.19.cloned.1.call-update) | async-done | bytes 3145744 | tf_op jit(solution)/shard_map/all_gather | solution.py:61
  778.0 4.5 convolution_convert_fusion
  782.5 4.4 reshape.429
  789.4 63.6 %while.28 = (s32[]{:T(128)}, f32[1024,2,96]{0,2,1:T(8,128)S(1)}, f32[1024,2,96]{0,2,1:T(8,128)}, f32[2,512,2,2,96]{1,0,4,3,2:T(2,128)}, bf16[2,512,2,2,96]{1,4,3...) while((s32[]{:T(128)}, f32[1024,2,96]{0,2,1:T(8,128)S(1)}, ...), condition=%wide.region_12.13_spmd.clone, body=%wide.region_10.12_spmd.clone.sunk | while | flops 2047998976 | bytes 74926256 | solution.py:291
  792.6 3.5 fusion.129
  796.1 4.2 fusion.126
  805.9 15.0 %dynamic_update_slice.20 = f32[2,512,2,2,96]{1,0,4,3,2:T(2,128)} dynamic-update-slice(f32[2,512,2,2,96]{1,0,4,3,2:T(2,128)} %get-tuple-element.557, f32[1,512,2,2,96]{1,0,4,3,2:T(1,128)S(1)} %copy.86, s32[]{:T(128)S(6)} %copy.103, s32[]{:T(128)} %constant.42.clone.1..sunk, s32[]{:T(128)} %constant.42.clone.1..sunk, s32[]{:T(128)} %constant.42.clone.1..sunk, s32[]{:T(128)} %constant.42.clone.1..sunk) | dynamic-update-slice | bytes 1572868 | tf_op jit(solution)/shard_map/while/body/jit(dynamic_update_index_in_dim)/dynamic_update_slice | solution.py:291
  823.6 4.6 fusion.129
  828.2 4.2 fusion.126
  838.0 15.0 %dynamic_update_slice.20 = f32[2,512,2,2,96]{1,0,4,3,2:T(2,128)} dynamic-update-slice(f32[2,512,2,2,96]{1,0,4,3,2:T(2,128)} %get-tuple-element.557, f32[1,512,2,2,96]{1,0,4,3,2:T(1,128)S(1)} %copy.86, s32[]{:T(128)S(6)} %copy.103, s32[]{:T(128)} %constant.42.clone.1..sunk, s32[]{:T(128)} %constant.42.clone.1..sunk, s32[]{:T(128)} %constant.42.clone.1..sunk, s32[]{:T(128)} %constant.42.clone.1..sunk) | dynamic-update-slice | bytes 1572868 | tf_op jit(solution)/shard_map/while/body/jit(dynamic_update_index_in_dim)/dynamic_update_slice | solution.py:291
  853.1 3.2 reshape.415
  860.1 4.7 fusion.67
  866.0 5.2 fusion.82
  871.3 6.8 fusion.81
  881.0 2.6 maximum_bitcast_fusion.2
  883.5 54.5 %reduce-scatter.21.cloned.1.call-done = f32[192,2,1024]{2,0,1:T(8,128)} async-done(((f32[1536,2,1024]{2,0,1:T(8,128)}), f32[192,2,1024]{2,0,1:T(8,128)}) %reduce-scatter.21.cloned.1.call-update) | async-done | bytes 1572880 | tf_op jit(solution)/shard_map/reduce_scatter | solution.py:322
  938.0 3.8 copy.53
  941.8 109.3 %reduce-scatter.17.cloned.1.call-done = f32[256,1536]{1,0:T(8,128)} async-done(((f32[1024,1536]{1,0:T(8,128)}), f32[256,1536]{1,0:T(8,128)}) %reduce-scatter.17.cloned.1.call-update) | async-done | bytes 1572880 | tf_op jit(solution)/shard_map/reduce_scatter | solution.py:65
  1052.9 41.0 %all-reduce = (f32[1,2,1536]{2,1,0:T(2,128)}, f32[1,4]{1,0:T(1,128)S(1)}) all-reduce(f32[1,2,1536]{2,1,0:T(2,128)S(1)} %maximum_bitcast_fusion.1, f32[1,4]{1,0:T(1,128)S(1)} %maximum_bitcast_fusion.2), channel_id=1, replica_groups=mesh['dp'=8,'tensor'=4] {'dp','tensor'}, use_global_device_ids=true, to_apply=%region_21.22 | all-reduce | flops 3076 | bytes 24608 | tf_op jit(solution)/shard_map/psum | solution.py:331
  1094.3 3.4 subtract_add_fusion
  1098.3 57.8 %reduce-scatter.19.cloned.1.call-done = f32[192,768]{1,0:T(8,128)} async-done(((f32[1536,768]{1,0:T(8,128)}), f32[192,768]{1,0:T(8,128)}) %reduce-scatter.19.cloned.1.call-update) | async-done | bytes 589840 | tf_op jit(solution)/shard_map/reduce_scatter | solution.py:321
  (160 shorter events, 60.7 us)
Async XLA Ops:
  7.2 7.1 copy-start.13
  7.2 7.2 copy-start.10
  7.2 34.5 %all-gather.21.cloned.1.call-start = ((), (), s32[]{:S(2)}) async-start(), calls=%async_computation.19 | async-start | bytes 2654208 | tf_op jit(solution)/shard_map/all_gather | solution.py:94
  7.9 99.4 %all-gather.13.cloned.1.call-start = ((), (), s32[]{:S(2)}) async-start(), calls=%async_computation.8 | async-start | bytes 3932160 | tf_op jit(solution)/shard_map/all_gather | solution.py:53
  8.8 5.6 copy-start.14
  8.8 245.4 %copy-start.16 = (f32[1536]{0:T(1024)}, f32[1536]{0:T(1024)S(1)}, u32[]{:S(2)}) copy-start(f32[1536]{0:T(1024)S(1)} %get-tuple-element.265) | copy-start | bytes 18436
  11.0 101.7 %copy-start.18 = (f32[256]{0:T(256)}, f32[256]{0:T(256)S(1)}, u32[]{:S(2)}) copy-start(f32[256]{0:T(256)S(1)} %get-tuple-element.347) | copy-start | bytes 3076
  13.5 122.0 %all-gather.23.cloned.1.call-start = ((), (), s32[]{:S(2)}) async-start(), calls=%async_computation.20 | async-start | bytes 1327104 | tf_op jit(solution)/shard_map/all_gather | solution.py:96
  14.2 236.8 %reduce-scatter.11.cloned.1.call-start = ((), (), s32[]{:S(2)}) async-start(), calls=%async_computation.9 | async-start | bytes 7864320 | tf_op jit(solution)/shard_map/reduce_scatter | solution.py:57
  15.8 98.0 %copy-start.4 = (f32[1024,48]{0,1:T(8,128)}, f32[1024,48]{0,1:T(8,128)S(1)}, u32[]{:S(2)}) copy-start(f32[1024,48]{0,1:T(8,128)S(1)} %get-tuple-element.345) | copy-start | bytes 589828
  135.4 6.0 copy-start.6
  141.5 109.6 %copy-start = (f32[256,1536]{1,0:T(8,128)S(1)}, f32[256,1536]{1,0:T(8,128)}, u32[]{:S(2)}) copy-start(f32[256,1536]{1,0:T(8,128)} %param.13) | copy-start | bytes 4718596
  141.5 157.4 %all-gather.25.cloned.1.call-start = ((), (), s32[]{:S(2)}) async-start(), calls=%async_computation.21 | async-start | bytes 7077888 | tf_op jit(solution)/shard_map/all_gather | solution.py:95
  142.1 222.3 %all-gather.15.cloned.1.call-start = ((), (), s32[]{:S(2)}) async-start(), calls=%async_computation.10 | async-start | bytes 3932160 | tf_op jit(solution)/shard_map/all_gather | solution.py:53
  253.6 1.1 copy-start.2
  254.2 61.1 %copy-start.20 = (f32[256]{0:T(256)}, f32[256]{0:T(256)S(1)}, u32[]{:S(2)}) copy-start(f32[256]{0:T(256)S(1)} %get-tuple-element.349) | copy-start | bytes 3076
  255.8 172.3 %all-gather.17.cloned.1.call-start = ((), (), s32[]{:S(2)}) async-start(), calls=%async_computation.12 | async-start | bytes 3932160 | tf_op jit(solution)/shard_map/all_gather | solution.py:61
  256.6 204.5 %all-gather.27.cloned.1.call-start = ((), (), s32[]{:S(2)}) async-start(), calls=%async_computation.22 | async-start | bytes 3538944 | tf_op jit(solution)/shard_map/all_gather | solution.py:97
  257.3 337.6 %reduce-scatter.15.cloned.1.call-start = ((), (), s32[]{:S(2)}) async-start(), calls=%async_computation.13 | async-start | bytes 7864320 | tf_op jit(solution)/shard_map/reduce_scatter | solution.py:65
  471.3 1.3 copy-start.24
  471.3 2.0 copy-start.26
  484.0 224.4 %reduce-scatter.13.cloned.1.call-start = ((), (), s32[]{:S(2)}) async-start(), calls=%async_computation.11 | async-start | bytes 7864320 | tf_op jit(solution)/shard_map/reduce_scatter | solution.py:57
  484.3 6.4 copy-start.22
  489.3 1.4 copy-start.9
  496.1 98.8 %copy-start.3 = (f32[256,1536]{1,0:T(8,128)S(1)}, f32[256,1536]{1,0:T(8,128)}, u32[]{:S(2)}) copy-start(f32[256,1536]{1,0:T(8,128)} %copy-done.2) | copy-start | bytes 4718596
  496.2 212.2 %copy-start.8 = (bf16[256,1536]{1,0:T(8,128)(2,1)S(1)}, bf16[256,1536]{1,0:T(8,128)(2,1)}, u32[]{:S(2)}) copy-start(bf16[256,1536]{1,0:T(8,128)(2,1)} %param.21) | copy-start | bytes 2359300
  496.2 281.8 %all-gather.19.cloned.1.call-start = ((), (), s32[]{:S(2)}) async-start(), calls=%async_computation.14 | async-start | bytes 3932160 | tf_op jit(solution)/shard_map/all_gather | solution.py:61
  713.8 164.3 %reduce-scatter.25.cloned.1.call-start = ((), (), s32[]{:S(2)}) async-start(), calls=%async_computation.23 | async-start | bytes 7077888
  729.1 1.6 copy-start.25
  729.1 208.9 %reduce-scatter.21.cloned.1.call-start = ((), (), s32[]{:S(2)}) async-start(), calls=%async_computation.17 | async-start | bytes 14155776 | tf_op jit(solution)/shard_map/reduce_scatter | solution.py:322
  742.4 35.6 %copy-start.12 = (bf16[1,1536,384]{2,1,0:T(8,128)(2,1)S(1)}, bf16[1,1536,384]{2,1,0:T(8,128)(2,1)}, u32[]{:S(2)}) copy-start(bf16[1,1536,384]{2,1,0:T(8,128)(2,1)} %all-gather.23.cloned.1.call-done) | copy-start | bytes 3538948
  742.4 308.6 %reduce-scatter.17.cloned.1.call-start = ((), (), s32[]{:S(2)}) async-start(), calls=%async_computation.15 | async-start | bytes 7864320 | tf_op jit(solution)/shard_map/reduce_scatter | solution.py:65
  853.1 3.2 copy-start.5
  853.1 3.2 copy-start.11
  857.9 2.2 copy-start.23
  864.8 1.2 copy-start.7
  864.8 233.5 %reduce-scatter.23.cloned.1.call-start = ((), (), s32[]{:S(2)}) async-start(), calls=%async_computation.18 | async-start | bytes 2654208 | tf_op jit(solution)/shard_map/reduce_scatter | solution.py:323
  871.2 284.9 %reduce-scatter.19.cloned.1.call-start = ((), (), s32[]{:S(2)}) async-start(), calls=%async_computation.16 | async-start | bytes 5308416 | tf_op jit(solution)/shard_map/reduce_scatter | solution.py:321
  878.1 2.9 copy-start.17
  878.1 172.9 %copy-start.1 = (f32[256,1536]{1,0:T(8,128)S(1)}, f32[256,1536]{1,0:T(8,128)}, u32[]{:S(2)}) copy-start(f32[256,1536]{1,0:T(8,128)} %param.13) | copy-start | bytes 4718596
  878.1 172.9 %copy-start.15 = (f32[1536]{0:T(1024)S(1)}, f32[1536]{0:T(1024)}, u32[]{:S(2)}) copy-start(f32[1536]{0:T(1024)} %copy-done.14) | copy-start | bytes 18436
  878.1 172.9 %copy-start.19 = (f32[256]{0:T(256)S(1)}, f32[256]{0:T(256)}, u32[]{:S(2)}) copy-start(f32[256]{0:T(256)} %copy-done.18) | copy-start | bytes 3076
  938.0 156.4 %copy-start.21 = (f32[256]{0:T(256)S(1)}, f32[256]{0:T(256)}, u32[]{:S(2)}) copy-start(f32[256]{0:T(256)} %get-tuple-element.346) | copy-start | bytes 3076
Sparse Core Ops, SparseCore 0:
  9.9 31.7 all-gather.20
  43.8 63.4 all-gather.12
  109.2 22.7 all-gather.22
  141.6 109.3 reduce-scatter.10
  252.8 46.0 all-gather.24
  300.9 63.4 all-gather.14
  366.0 62.1 all-gather.16
  430.0 30.9 all-gather.26
  484.2 110.7 reduce-scatter.14
  597.1 111.2 reduce-scatter.12
  713.9 64.0 all-gather.18
  781.2 60.3 reduce-scatter.24
  845.6 92.3 reduce-scatter.20
  940.2 110.7 reduce-scatter.16
  1055.2 43.1 reduce-scatter.22
  1102.2 53.8 reduce-scatter.18
where the time goes:
time: 1170 us; the launch traced here: 1160 us
  waiting for transfers between devices  846 us (72%)
  matrix products  126 us (11%)
  local copies, waits for them, and re-layouts  84.5 us (7%)
  other arithmetic  49.1 us (4%)
  blocking collectives  41 us (4%)
  between operations  14.6 us (1%)
    reduce_scatter x2, waiting for transfers between devices, collect_rows(): return lax.psum_scatter(values, 'tensor', scatter_dimension=0, tiled=True)  219 us
    reduce_scatter x2, waiting for transfers between devices, collect_grads(): return lax.psum_scatter(values, 'tensor', scatter_dimension=0, tiled=True)  208 us
    all_gather x2, waiting for transfers between devices, spread_rows(): return lax.all_gather(values, 'tensor', axis=0, tiled=True)  115 us
    all_gather x2, waiting for transfers between devices, spread_grads(): return lax.all_gather(values, 'tensor', axis=0, tiled=True)  87.5 us
    reduce_scatter x1, waiting for transfers between devices, per_device(): lax.psum_scatter(grad_qkv_w, 'dp', scatter_dimension=0, tiled=True)  57.8 us
    reduce_scatter x1, waiting for transfers between devices, per_device(): lax.psum_scatter(grad_gu_w, 'dp', scatter_dimension=0, tiled=True)  54.5 us
    all_gather x1, waiting for transfers between devices, per_device(): lax.all_gather(w_gate_up[layer_index], 'dp', axis=0, tiled=True)  41.5 us
    psum x1, blocking collectives, per_device(): lax.psum((jnp.stack(gain_list), jnp.stack(stat_rows)), ('dp', 'tensor'))  41 us
  transfers between devices with their start and end apart: 16, of which 14 were waited for; matrix products, arithmetic and copies ran while one was open for 19% of the time, Pallas kernels for 0%

commit v1 on v0

--- a/solution.py
+++ b/solution.py
@@ -8,6 +8,18 @@
 HEAD_WIDTH = 96
 norm_eps = 1e-05
 rope_base = 100000.0
+
+
+def gather_by_bits(x, axis, dim):
+    ways, here = (lax.axis_size(axis), lax.axis_index(axis))
+    grown, reach = (x, 1)
+    while reach < ways:
+        theirs = lax.ppermute(grown, axis, [(d, d ^ reach) for d in range(ways)])
+        mine_first = jnp.concatenate([grown, theirs], axis=dim)
+        theirs_first = jnp.concatenate([theirs, grown], axis=dim)
+        grown = jnp.where(here & reach == 0, mine_first, theirs_first)
+        reach = 2 * reach
+    return grown
 
 
 def rope_tables(position, head_dim):
@@ -50,7 +62,7 @@
 
 
 def spread_rows(values):
-    return lax.all_gather(values, "tensor", axis=0, tiled=True)
+    return gather_by_bits(values, "tensor", 0)
 
 
 def collect_rows(values):

time: 1170 us -> 1260 us (1.077)
  waiting for transfers between devices: 846 us -> 915 us
    ppermute x0 -> x4, waiting for transfers between devices: none -> 183 us  [gather_by_bits(): theirs = lax.ppermute(grown, axis, [(d, d ^ reach) for d in range(ways)])]
    all_gather x2, waiting for transfers between devices: 115 us -> 44 us  [refold(): lax.all_gather(normed_local, 'tensor', axis=0, tiled=True)]
    reduce_scatter x1, waiting for transfers between devices: 54.5 us -> 91 us  [per_device(): lax.psum_scatter(grad_gu_w, 'dp', scatter_dimension=0, tiled=True)]
    all_gather x2, waiting for transfers between devices: 87.5 us -> 51.8 us  [spread_grads(): return lax.all_gather(values, 'tensor', axis=0, tiled=True)]
    all_gather x1, waiting for transfers between devices: 25.8 us -> 0.01 us  [per_device(): lax.all_gather(w_qkv[layer_index], 'dp', axis=0, tiled=True)]
    all_gather x1, waiting for transfers between devices: 41.5 us -> 20.1 us  [per_device(): lax.all_gather(w_gate_up[layer_index], 'dp', axis=0, tiled=True)]
    unnamed x17, waiting for transfers between devices: 3.49 us -> 24.7 us
    all_gather x1, waiting for transfers between devices: 32.9 us -> 14.4 us  [per_device(): lax.all_gather(w_down[layer_index], 'dp', axis=0, tiled=True)]
  transfers between devices with their start and end apart: 16 -> 20, of which waited for: 14 -> 16; matrix products, arithmetic and copies ran while one was open for 19% -> 19% of each run, Pallas kernels for 0% -> 0%
where the time goes in v1:
time: 1260 us; the launch traced here: 1250 us
  waiting for transfers between devices  915 us (73%)
  matrix products  134 us (11%)
  local copies, waits for them, and re-layouts  85.1 us (7%)
  other arithmetic  47.4 us (4%)
  blocking collectives  41 us (3%)
  between operations  14.9 us (1%)
    reduce_scatter x2, waiting for transfers between devices, collect_rows(): return lax.psum_scatter(values, 'tensor', scatter_dimension=0, tiled=True)  220 us
    reduce_scatter x2, waiting for transfers between devices, collect_grads(): return lax.psum_scatter(values, 'tensor', scatter_dimension=0, tiled=True)  207 us
    ppermute x4, waiting for transfers between devices, gather_by_bits(): theirs = lax.ppermute(grown, axis, [(d, d ^ reach) for d in range(ways)])  183 us
    reduce_scatter x1, waiting for transfers between devices, per_device(): lax.psum_scatter(grad_gu_w, 'dp', scatter_dimension=0, tiled=True)  91 us
    reduce_scatter x1, waiting for transfers between devices, per_device(): lax.psum_scatter(grad_qkv_w, 'dp', scatter_dimension=0, tiled=True)  57.8 us
    all_gather x2, waiting for transfers between devices, spread_grads(): return lax.all_gather(values, 'tensor', axis=0, tiled=True)  51.8 us
    all_gather x2, waiting for transfers between devices, refold(): lax.all_gather(normed_local, 'tensor', axis=0, tiled=True)  44 us
    psum x1, blocking collectives, per_device(): lax.psum((jnp.stack(gain_list), jnp.stack(stat_rows)), ('dp', 'tensor'))  41 us
  transfers between devices with their start and end apart: 20, of which 16 were waited for; matrix products, arithmetic and copies ran while one was open for 19% of the time, Pallas kernels for 0%

profile of v1, /device:TPU:0, one launch (start us, length us, event | category | flops | bytes accessed | tf_op | source)
XLA Modules:
  0.0 1249.9 jit_solution(9835473197070400610)
XLA Ops:
  13.1 3.1 collective-permute-start
  16.2 17.5 %collective-permute-done = bf16[256,1536]{1,0:T(8,128)(2,1)S(1)} collective-permute-done((bf16[256,1536]{1,0:T(8,128)(2,1)S(1)}, bf16[256,1536]{1,0:T(8,128)(2,1)S(1)}, u32[]{:S(2)}, u32[]{:S(2)}) %collective-permute-start) | collective-permute-done | bytes 786464 | tf_op jit(solution)/shard_map/ppermute | solution.py:17
  38.9 65.9 %collective-permute-done.1 = bf16[512,1536]{1,0:T(8,128)(2,1)} collective-permute-done((bf16[512,1536]{1,0:T(8,128)(2,1)S(1)}, bf16[512,1536]{1,0:T(8,128)(2,1)}, u32[]{:S(2)}, u32[]{:S(2)}) %collective-permute-start.1) | collective-permute-done | bytes 1572896 | tf_op jit(solution)/shard_map/ppermute | solution.py:17
  104.8 5.4 fusion.61
  112.4 17.9 %while.27 = (s32[]{:T(128)}, bf16[2,512,2,2,96]{1,4,3,2,0:T(8,128)(2,1)}, f32[2,2,2,512]{3,2,1,0:T(2,128)S(1)}, s32[1024]{0:T(1024)S(1)}, s32[2,512]{1,0:T(2,128...) while((s32[]{:T(128)}, ...), condition=%wide.region_4.5_spmd, body=%wide.region_1.4_spmd.sunk | while | flops 832764928 | bytes 35219636 | solution.py:142
  117.5 3.1 fusion.130
  126.3 3.1 fusion.130
  132.6 6.0 fusion.85
  140.4 110.1 %reduce-scatter.11.cloned.1.call-done = f32[256,1536]{1,0:T(8,128)} async-done(((f32[1024,1536]{1,0:T(8,128)}), f32[256,1536]{1,0:T(8,128)}) %reduce-scatter.11.cloned.1.call-update) | async-done | bytes 1572880 | tf_op jit(solution)/shard_map/reduce_scatter | solution.py:69
  256.7 17.8 %collective-permute-done.2 = bf16[256,1536]{1,0:T(8,128)(2,1)S(1)} collective-permute-done((bf16[256,1536]{1,0:T(8,128)(2,1)S(1)}, bf16[256,1536]{1,0:T(8,128)(2,1)S(1)}, u32[]{:S(2)}, u32[]{:S(2)}) %collective-permute-start.2) | collective-permute-done | bytes 786464 | tf_op jit(solution)/shard_map/ppermute | solution.py:17
  278.2 20.1 %all-gather.25.cloned.1.call-done = bf16[1,1536,2,1024]{3,2,0,1:T(2,128)(2,1)} async-done(((bf16[1,192,2,1024]{3,2,0,1:T(2,128)(2,1)}), bf16[1,1536,2,1024]{3,2,0,1:T(2,128)(2,1)}) %all-gather.25.cloned.1.call-update) | async-done | bytes 6291472 | tf_op jit(solution)/shard_map/all_gather | solution.py:107
  298.3 16.6 %copy.45 = bf16[1,1536,2,1024]{1,3,2,0:T(8,128)(2,1)} copy(bf16[1,1536,2,1024]{3,2,0,1:T(2,128)(2,1)} %all-gather.25.cloned.1.call-done) | data formatting | bytes 12582912 | tf_op jit(solution)/shard_map/all_gather | solution.py:107
  314.9 81.7 %collective-permute-done.3 = bf16[512,1536]{1,0:T(8,128)(2,1)} collective-permute-done((bf16[512,1536]{1,0:T(8,128)(2,1)S(1)}, bf16[512,1536]{1,0:T(8,128)(2,1)}, u32[]{:S(2)}, u32[]{:S(2)}) %collective-permute-start.3) | collective-permute-done | bytes 1572896 | tf_op jit(solution)/shard_map/ppermute | solution.py:17
  396.6 12.7 %fusion.53 = f32[1024,2,1024]{0,2,1:T(8,128)} fusion(bf16[1,1536,2,1024]{1,3,2,0:T(8,128)(2,1)} %copy.45, bf16[512,1536]{1,0:T(8,128)(2,1)} %collective-permute-done.3, bf16[512,1536]{1,0:T(8,128)(2,1)S(1)} %maximum_select_fusion.4, pred[]{:T(512)S(6)} %eq.62), kind=kOutput, calls=%fused_computation.68 | convolution fusion | flops 6456606720 | bytes 17825792 | tf_op jit(solution)/shard_map/td,dcf->tcf/dot_general | solution.py:159
  409.3 14.4 %all-gather.27.cloned.1.call-done = bf16[1,1536,1024]{2,1,0:T(8,128)(2,1)} async-done(((bf16[1,192,1024]{2,1,0:T(8,128)(2,1)}), bf16[1,1536,1024]{2,1,0:T(8,128)(2,1)}) %all-gather.27.cloned.1.call-update) | async-done | bytes 3145744 | tf_op jit(solution)/shard_map/all_gather | solution.py:109
  423.7 10.3 multiply_bitcast_fusion.1
  436.0 10.7 fusion.55
  447.0 5.0 multiply_convert_fusion
  453.4 5.5 fusion.77
  459.7 98.0 %reduce-scatter.15.cloned.1.call-done = f32[256,1536]{1,0:T(8,128)} async-done(((f32[1024,1536]{1,0:T(8,128)}), f32[256,1536]{1,0:T(8,128)}) %reduce-scatter.15.cloned.1.call-update) | async-done | bytes 1572880 | tf_op jit(solution)/shard_map/reduce_scatter | solution.py:77
  561.0 110.2 %reduce-scatter.13.cloned.1.call-done = f32[256,1536]{1,0:T(8,128)} async-done(((f32[1024,1536]{1,0:T(8,128)}), f32[256,1536]{1,0:T(8,128)}) %reduce-scatter.13.cloned.1.call-update) | async-done | bytes 1572880 | tf_op jit(solution)/shard_map/reduce_scatter | solution.py:69
  671.3 5.5 multiply_reduce_fusion.2
  677.5 8.7 convolution_bitcast_fusion.1
  686.2 6.7 copy.69
  692.9 44.0 %all-gather.19.cloned.1.call-done = bf16[1024,1536]{1,0:T(8,128)(2,1)} async-done(((bf16[256,1536]{1,0:T(8,128)(2,1)}), bf16[1024,1536]{1,0:T(8,128)(2,1)}) %all-gather.19.cloned.1.call-update) | async-done | bytes 3145744 | tf_op jit(solution)/shard_map/all_gather | solution.py:83
  736.9 12.2 fusion.58
  749.3 51.8 %all-gather.15.cloned.1.call-done = bf16[1024,1536]{1,0:T(8,128)(2,1)} async-done(((bf16[256,1536]{1,0:T(8,128)(2,1)}), bf16[1024,1536]{1,0:T(8,128)(2,1)}) %all-gather.15.cloned.1.call-update) | async-done | bytes 3145744 | tf_op jit(solution)/shard_map/all_gather | solution.py:73
  801.1 4.6 convolution_convert_fusion
  805.6 4.5 reshape.429
  810.1 3.6 copy.50
  813.7 70.1 %while.28 = (s32[]{:T(128)}, f32[1024,2,96]{0,2,1:T(8,128)S(1)}, f32[1024,2,96]{0,2,1:T(8,128)}, f32[2,512,2,2,96]{1,0,4,3,2:T(2,128)}, bf16[2,512,2,2,96]{1,4,3...) while((s32[]{:T(128)}, f32[1024,2,96]{0,2,1:T(8,128)S(1)}, ...), condition=%wide.region_12.13_spmd.clone, body=%wide.region_10.12_spmd.clone.sunk | while | flops 2047998976 | bytes 133122368 | solution.py:303
  815.9 3.2 fusion.140
  823.9 15.0 %dynamic_update_slice.20 = f32[2,512,2,2,96]{1,0,4,3,2:T(2,128)} dynamic-update-slice(f32[2,512,2,2,96]{1,0,4,3,2:T(2,128)} %get-tuple-element.557, f32[1,512,2,2,96]{1,0,4,3,2:T(1,128)S(1)} %copy.86, s32[]{:T(128)} %get-tuple-element.554, s32[]{:T(128)} %constant.43.clone.1..sunk, s32[]{:T(128)} %constant.43.clone.1..sunk, s32[]{:T(128)} %constant.43.clone.1..sunk, s32[]{:T(128)} %constant.43.clone.1..sunk) | dynamic-update-slice | bytes 1572868 | tf_op jit(solution)/shard_map/while/body/jit(dynamic_update_index_in_dim)/dynamic_update_slice | solution.py:303
  838.9 3.2 fusion.142
  842.1 5.8 fusion.143
  849.9 3.2 fusion.140
  857.8 15.0 %dynamic_update_slice.20 = f32[2,512,2,2,96]{1,0,4,3,2:T(2,128)} dynamic-update-slice(f32[2,512,2,2,96]{1,0,4,3,2:T(2,128)} %get-tuple-element.557, f32[1,512,2,2,96]{1,0,4,3,2:T(1,128)S(1)} %copy.86, s32[]{:T(128)} %get-tuple-element.554, s32[]{:T(128)} %constant.43.clone.1..sunk, s32[]{:T(128)} %constant.43.clone.1..sunk, s32[]{:T(128)} %constant.43.clone.1..sunk, s32[]{:T(128)} %constant.43.clone.1..sunk) | dynamic-update-slice | bytes 1572868 | tf_op jit(solution)/shard_map/while/body/jit(dynamic_update_index_in_dim)/dynamic_update_slice | solution.py:303
  872.8 3.6 fusion.142
  876.5 7.3 fusion.143
  889.8 4.6 fusion.81
  895.5 5.2 fusion.97
  900.8 6.7 fusion.96
  907.6 21.0 %reduce-scatter.25.cloned.1.call-done = f32[192,1024]{1,0:T(8,128)} async-done(((f32[1536,1024]{1,0:T(8,128)}), f32[192,1024]{1,0:T(8,128)}) %reduce-scatter.25.cloned.1.call-update) | async-done | bytes 786448
  933.8 91.0 %reduce-scatter.21.cloned.1.call-done = f32[192,2,1024]{2,0,1:T(8,128)} async-done(((f32[1536,2,1024]{2,0,1:T(8,128)}), f32[192,2,1024]{2,0,1:T(8,128)}) %reduce-scatter.21.cloned.1.call-update) | async-done | bytes 1572880 | tf_op jit(solution)/shard_map/reduce_scatter | solution.py:334
  1024.8 3.9 copy.53
  1028.7 109.1 %reduce-scatter.17.cloned.1.call-done = f32[256,1536]{1,0:T(8,128)} async-done(((f32[1024,1536]{1,0:T(8,128)}), f32[256,1536]{1,0:T(8,128)}) %reduce-scatter.17.cloned.1.call-update) | async-done | bytes 1572880 | tf_op jit(solution)/shard_map/reduce_scatter | solution.py:77
  1139.7 41.0 %all-reduce = (f32[1,2,1536]{2,1,0:T(2,128)}, f32[1,4]{1,0:T(1,128)S(1)}) all-reduce(f32[1,2,1536]{2,1,0:T(2,128)S(1)} %maximum_bitcast_fusion.1, f32[1,4]{1,0:T(1,128)S(1)} %maximum_bitcast_fusion.2), channel_id=1, replica_groups=mesh['dp'=8,'tensor'=4] {'dp','tensor'}, use_global_device_ids=true, to_apply=%region_21.22 | all-reduce | flops 3076 | bytes 24608 | tf_op jit(solution)/shard_map/psum | solution.py:343
  1185.2 57.8 %reduce-scatter.19.cloned.1.call-done = f32[192,768]{1,0:T(8,128)} async-done(((f32[1536,768]{1,0:T(8,128)}), f32[192,768]{1,0:T(8,128)}) %reduce-scatter.19.cloned.1.call-update) | async-done | bytes 589840 | tf_op jit(solution)/shard_map/reduce_scatter | solution.py:333
  (208 shorter events, 79.0 us)
Async XLA Ops:
  7.2 97.6 %all-gather.21.cloned.1.call-start = ((), (), s32[]{:S(2)}) async-start(), calls=%async_computation.19 | async-start | bytes 2654208 | tf_op jit(solution)/shard_map/all_gather | solution.py:106
  7.9 124.7 %all-gather.23.cloned.1.call-start = ((), (), s32[]{:S(2)}) async-start(), calls=%async_computation.20 | async-start | bytes 1327104 | tf_op jit(solution)/shard_map/all_gather | solution.py:108
  9.4 25.0 %copy-start.26 = (f32[1536]{0:T(1024)}, f32[1536]{0:T(1024)S(1)}, u32[]{:S(2)}) copy-start(f32[1536]{0:T(1024)S(1)} %get-tuple-element.266) | copy-start | bytes 18436
  11.0 26.3 %copy-start.25 = (s32[1024]{0:T(1024)S(1)}, s32[1024]{0:T(1024)}, u32[]{:S(2)}) copy-start(s32[1024]{0:T(1024)} %param.20) | copy-start | bytes 12292
  11.0 26.4 %copy-start.20 = (s32[1024]{0:T(1024)S(1)}, s32[1024]{0:T(1024)}, u32[]{:S(2)}) copy-start(s32[1024]{0:T(1024)} %param.19) | copy-start | bytes 12292
  11.5 25.9 %copy-start.31 = (f32[256]{0:T(256)}, f32[256]{0:T(256)S(1)}, u32[]{:S(2)}) copy-start(f32[256]{0:T(256)S(1)} %get-tuple-element.347) | copy-start | bytes 3076
  13.1 97.0 %copy-start.11 = (bf16[256,1536]{1,0:T(8,128)(2,1)}, bf16[256,1536]{1,0:T(8,128)(2,1)S(1)}, u32[]{:S(2)}) copy-start(bf16[256,1536]{1,0:T(8,128)(2,1)S(1)} %multiply_convert_fusion.2) | copy-start | bytes 2359300
  13.1 20.6 %collective-permute-start = (bf16[256,1536]{1,0:T(8,128)(2,1)S(1)}, bf16[256,1536]{1,0:T(8,128)(2,1)S(1)}, u32[]{:S(2)}, u32[]{:S(2)}) collective-permute-start(bf16[256,1536]{1,0:T(8,128)(2,1)S(1)} %multiply_convert_fusion.2), channel_id=1, source_target_pairs={{0,1},{1,0},{2,3},{3,2},{4,5},{5,4},{6,7},{7,6},{8,9},{9,8},{10,11... | collective-permute-start | bytes 2359304 | tf_op jit(solution)/shard_map/ppermute | solution.py:17
  34.4 70.4 %collective-permute-start.1 = (bf16[512,1536]{1,0:T(8,128)(2,1)S(1)}, bf16[512,1536]{1,0:T(8,128)(2,1)}, u32[]{:S(2)}, u32[]{:S(2)}) collective-permute-start(bf16[512,1536]{1,0:T(8,128)(2,1)S(1)} %maximum_select_fusion.3), channel_id=1, source_target_pairs={{0,2},{1,3},{2,0},{3,1},{4,6},{5,7},{6,4},{7,5},{8,10},{9,11},{10,... | collective-permute-start | bytes 4718600 | tf_op jit(solution)/shard_map/ppermute | solution.py:17
  37.3 213.2 %reduce-scatter.11.cloned.1.call-start = ((), (), s32[]{:S(2)}) async-start(), calls=%async_computation.8 | async-start | bytes 7864320 | tf_op jit(solution)/shard_map/reduce_scatter | solution.py:69
  38.9 71.7 %copy-start.14 = (f32[1024,48]{0,1:T(8,128)}, f32[1024,48]{0,1:T(8,128)S(1)}, u32[]{:S(2)}) copy-start(f32[1024,48]{0,1:T(8,128)S(1)} %get-tuple-element.345) | copy-start | bytes 589828
  130.3 8.2 copy-start.6
  130.3 8.2 copy-start.28
  132.5 6.0 copy-start.16
  138.6 111.9 %copy-start.2 = (f32[256,1536]{1,0:T(8,128)S(1)}, f32[256,1536]{1,0:T(8,128)}, u32[]{:S(2)}) copy-start(f32[256,1536]{1,0:T(8,128)} %param.13) | copy-start | bytes 4718596
  138.6 159.7 %all-gather.25.cloned.1.call-start = ((), (), s32[]{:S(2)}) async-start(), calls=%async_computation.21 | async-start | bytes 7077888 | tf_op jit(solution)/shard_map/all_gather | solution.py:107
  139.2 270.1 %all-gather.13.cloned.1.call-start = ((), (), s32[]{:S(2)}) async-start(), calls=%async_computation.10 | async-start | bytes 3932160 | tf_op jit(solution)/shard_map/all_gather | solution.py:73
  139.8 284.0 %all-gather.27.cloned.1.call-start = ((), (), s32[]{:S(2)}) async-start(), calls=%async_computation.22 | async-start | bytes 3538944 | tf_op jit(solution)/shard_map/all_gather | solution.py:109
  140.3 417.3 %reduce-scatter.15.cloned.1.call-start = ((), (), s32[]{:S(2)}) async-start(), calls=%async_computation.11 | async-start | bytes 7864320 | tf_op jit(solution)/shard_map/reduce_scatter | solution.py:77
  255.1 59.8 %copy-start.12 = (bf16[256,1536]{1,0:T(8,128)(2,1)}, bf16[256,1536]{1,0:T(8,128)(2,1)S(1)}, u32[]{:S(2)}) copy-start(bf16[256,1536]{1,0:T(8,128)(2,1)S(1)} %multiply_convert_fusion.1) | copy-start | bytes 2359300
  255.1 19.4 %collective-permute-start.2 = (bf16[256,1536]{1,0:T(8,128)(2,1)S(1)}, bf16[256,1536]{1,0:T(8,128)(2,1)S(1)}, u32[]{:S(2)}, u32[]{:S(2)}) collective-permute-start(bf16[256,1536]{1,0:T(8,128)(2,1)S(1)} %multiply_convert_fusion.1), channel_id=1, source_target_pairs={{0,1},{1,0},{2,3},{3,2},{4,5},{5,4},{6,7},{7,6},{8,9},{9,8},{10,11... | collective-permute-start | bytes 2359304 | tf_op jit(solution)/shard_map/ppermute | solution.py:17
  275.2 121.4 %collective-permute-start.3 = (bf16[512,1536]{1,0:T(8,128)(2,1)S(1)}, bf16[512,1536]{1,0:T(8,128)(2,1)}, u32[]{:S(2)}, u32[]{:S(2)}) collective-permute-start(bf16[512,1536]{1,0:T(8,128)(2,1)S(1)} %maximum_select_fusion.4), channel_id=1, source_target_pairs={{0,2},{1,3},{2,0},{3,1},{4,6},{5,7},{6,4},{7,5},{8,10},{9,11},{10,... | collective-permute-start | bytes 4718600 | tf_op jit(solution)/shard_map/ppermute | solution.py:17
  446.8 224.5 %reduce-scatter.13.cloned.1.call-start = ((), (), s32[]{:S(2)}) async-start(), calls=%async_computation.9 | async-start | bytes 7864320 | tf_op jit(solution)/shard_map/reduce_scatter | solution.py:69
  447.0 6.4 copy-start.35
  458.9 98.8 %copy-start.5 = (f32[256,1536]{1,0:T(8,128)S(1)}, f32[256,1536]{1,0:T(8,128)}, u32[]{:S(2)}) copy-start(f32[256,1536]{1,0:T(8,128)} %copy-done.4) | copy-start | bytes 4718596
  458.9 212.4 %copy-start.18 = (bf16[256,1536]{1,0:T(8,128)(2,1)S(1)}, bf16[256,1536]{1,0:T(8,128)(2,1)}, u32[]{:S(2)}) copy-start(bf16[256,1536]{1,0:T(8,128)(2,1)} %param.21) | copy-start | bytes 2359300
  458.9 278.0 %all-gather.19.cloned.1.call-start = ((), (), s32[]{:S(2)}) async-start(), calls=%async_computation.16 | async-start | bytes 3932160 | tf_op jit(solution)/shard_map/all_gather | solution.py:83
  459.6 341.5 %all-gather.15.cloned.1.call-start = ((), (), s32[]{:S(2)}) async-start(), calls=%async_computation.12 | async-start | bytes 3932160 | tf_op jit(solution)/shard_map/all_gather | solution.py:73
  676.8 224.0 %all-gather.17.cloned.1.call-start = ((), (), s32[]{:S(2)}) async-start(), calls=%async_computation.14 | async-start | bytes 3932160 | tf_op jit(solution)/shard_map/all_gather | solution.py:83
  677.5 251.0 %reduce-scatter.25.cloned.1.call-start = ((), (), s32[]{:S(2)}) async-start(), calls=%async_computation.23 | async-start | bytes 7077888
  692.9 332.0 %reduce-scatter.21.cloned.1.call-start = ((), (), s32[]{:S(2)}) async-start(), calls=%async_computation.17 | async-start | bytes 14155776 | tf_op jit(solution)/shard_map/reduce_scatter | solution.py:334
  749.2 51.9 %copy-start.22 = (bf16[1,1536,384]{2,1,0:T(8,128)(2,1)S(1)}, bf16[1,1536,384]{2,1,0:T(8,128)(2,1)}, u32[]{:S(2)}) copy-start(bf16[1,1536,384]{2,1,0:T(8,128)(2,1)} %all-gather.23.cloned.1.call-done) | copy-start | bytes 3538948
  749.2 388.7 %reduce-scatter.17.cloned.1.call-start = ((), (), s32[]{:S(2)}) async-start(), calls=%async_computation.13 | async-start | bytes 7864320 | tf_op jit(solution)/shard_map/reduce_scatter | solution.py:77
  805.6 8.1 copy-start.7
  805.6 8.1 copy-start.29
  815.9 3.3 copy-start
  842.1 5.8 copy-start.8
  849.8 3.3 copy-start
  872.8 3.6 copy-start.10
  876.5 7.3 copy-start.8
  894.4 290.7 %reduce-scatter.23.cloned.1.call-start = ((), (), s32[]{:S(2)}) async-start(), calls=%async_computation.18 | async-start | bytes 2654208 | tf_op jit(solution)/shard_map/reduce_scatter | solution.py:335
  900.7 342.2 %reduce-scatter.19.cloned.1.call-start = ((), (), s32[]{:S(2)}) async-start(), calls=%async_computation.15 | async-start | bytes 5308416 | tf_op jit(solution)/shard_map/reduce_scatter | solution.py:333
  907.5 23.7 %copy-start.30 = (f32[1536]{0:T(1024)S(1)}, f32[1536]{0:T(1024)}, u32[]{:S(2)}) copy-start(f32[1536]{0:T(1024)} %get-tuple-element.262) | copy-start | bytes 18436
  907.5 230.4 %copy-start.3 = (f32[256,1536]{1,0:T(8,128)S(1)}, f32[256,1536]{1,0:T(8,128)}, u32[]{:S(2)}) copy-start(f32[256,1536]{1,0:T(8,128)} %param.13) | copy-start | bytes 4718596
  907.5 230.3 %copy-start.27 = (f32[1536]{0:T(1024)S(1)}, f32[1536]{0:T(1024)}, u32[]{:S(2)}) copy-start(f32[1536]{0:T(1024)} %copy-done.26) | copy-start | bytes 18436
  907.5 230.3 %copy-start.32 = (f32[256]{0:T(256)S(1)}, f32[256]{0:T(256)}, u32[]{:S(2)}) copy-start(f32[256]{0:T(256)} %copy-done.31) | copy-start | bytes 3076
  1024.8 156.4 %copy-start.13 = (f32[256,1536]{1,0:T(8,128)S(1)}, f32[256,1536]{1,0:T(8,128)}, u32[]{:S(2)}) copy-start(f32[256,1536]{1,0:T(8,128)} %get-tuple-element.338) | copy-start | bytes 4718596
  1024.8 156.4 %copy-start.34 = (f32[256]{0:T(256)S(1)}, f32[256]{0:T(256)}, u32[]{:S(2)}) copy-start(f32[256]{0:T(256)} %get-tuple-element.346) | copy-start | bytes 3076
  (18 other events, 32.3 us)
Sparse Core Ops, SparseCore 0:
  9.9 31.7 all-gather.20
  43.5 24.0 all-gather.22
  138.7 111.7 reduce-scatter.10
  252.2 46.0 all-gather.24
  299.7 89.3 all-gather.12
  390.9 32.8 all-gather.26
  446.9 110.7 reduce-scatter.14
  560.0 111.2 reduce-scatter.12
  672.8 64.0 all-gather.18
  738.9 62.1 all-gather.14
  802.7 62.1 all-gather.16
  868.1 60.3 reduce-scatter.24
  932.4 92.3 reduce-scatter.20
  1027.1 110.7 reduce-scatter.16
  1142.0 43.1 reduce-scatter.22
  1189.0 53.8 reduce-scatter.18
